TPU v7x, 32 devices: a whole 2x2x4 slice. The times are simulated.
32 devices in a mesh: space: 4 (over z), energy: 8 (over y, x, core).
Axes of the slice: x: 2, y: 2, z: 4, core: 2. Of those that a mesh axis runs over, the one named last changes fastest.
Arguments:
- retain: float32 [8, 8], P('space', 'energy'), may hold values from 0.12 to 0.89
- hopping: float32 [8, 8, 2, 128, 128], P('space', 'energy'), may hold values from -0.125 to 0.125
- source: float32 [8, 8, 2, 128, 128], P('space', 'energy'), may hold values from -0.9 to 0.9
- screened: float32 [8, 8, 2, 16384], P('space', None, None, 'energy'), may hold values from -2 to 2
Outputs:
- greens: float32 [8, 8, 2, 128, 128], P('space', 'energy')
- self_energy: float32 [8, 8, 2, 16384], P('space', None, None, 'energy')
All inputs are finite; a program needn't handle non-finite values.
Results may differ from a plain program's by a relative error of at most 0.0001.
Values sent between devices are 32-bit elements; how exact they have to be, the bound alone decides.
A program may use at most 64 MiB of HBM per device.

v0:
```python
import math
import jax
import jax.numpy as jnp
from jax import lax
from jax.sharding import PartitionSpec as P

EXACT_PRECISION = lax.Precision.HIGHEST


def shifted(value, axis, steps):
    count = lax.axis_size(axis)
    initial, last = (max(0, -steps), min(count, count - steps))
    return lax.ppermute(value, axis, [(source, source + steps) for source in range(initial, last)])


def build_coupler(retain_slab, hop_slab):
    size = hop_slab.shape[-1]
    diagonal_ones = jnp.eye(size, dtype=jnp.float32)
    factor = retain_slab[:, None, None]
    return jnp.stack([factor * (diagonal_ones + hop_slab[:, 0]), factor * hop_slab[:, 1]], axis=1)


def complex_product(left_matrix, right_matrix):
    real_component = jnp.einsum(
        "eij,ejk->eik", left_matrix[:, 0], right_matrix[:, 0], precision=EXACT_PRECISION
    ) - jnp.einsum("eij,ejk->eik", left_matrix[:, 1], right_matrix[:, 1], precision=EXACT_PRECISION)
    imaginary_component = jnp.einsum(
        "eij,ejk->eik", left_matrix[:, 0], right_matrix[:, 1], precision=EXACT_PRECISION
    ) + jnp.einsum("eij,ejk->eik", left_matrix[:, 1], right_matrix[:, 0], precision=EXACT_PRECISION)
    return jnp.stack([real_component, imaginary_component], axis=1)


def times_dagger(left_matrix, right_matrix):
    real_component = jnp.einsum(
        "eij,ekj->eik", left_matrix[:, 0], right_matrix[:, 0], precision=EXACT_PRECISION
    ) + jnp.einsum("eij,ekj->eik", left_matrix[:, 1], right_matrix[:, 1], precision=EXACT_PRECISION)
    imaginary_component = jnp.einsum(
        "eij,ekj->eik", left_matrix[:, 1], right_matrix[:, 0], precision=EXACT_PRECISION
    ) - jnp.einsum("eij,ekj->eik", left_matrix[:, 0], right_matrix[:, 1], precision=EXACT_PRECISION)
    return jnp.stack([real_component, imaginary_component], axis=1)


def sandwich(coupler, middle):
    return times_dagger(complex_product(coupler, middle), coupler)


def fourier_tables(length, columns):
    rows_index = jnp.arange(length, dtype=jnp.int32)[:, None]
    cols_index = jnp.arange(columns, dtype=jnp.int32)[None, :]
    phases = (rows_index * cols_index % length).astype(jnp.float32) * (2.0 * math.pi / length)
    return (jnp.cos(phases), jnp.sin(phases))


def forward_transform(series, cosine_lookup, sine_lookup):
    real_input = series[:, :, 0]
    imaginary_input = series[:, :, 1]
    real_component = jnp.einsum(
        "gt,itx->igx", cosine_lookup, real_input, precision=EXACT_PRECISION
    ) + jnp.einsum("gt,itx->igx", sine_lookup, imaginary_input, precision=EXACT_PRECISION)
    imaginary_component = jnp.einsum(
        "gt,itx->igx", cosine_lookup, imaginary_input, precision=EXACT_PRECISION
    ) - jnp.einsum("gt,itx->igx", sine_lookup, real_input, precision=EXACT_PRECISION)
    return jnp.stack([real_component, imaginary_component], axis=2)


def body(retain, hopping, source, screened):
    couplers = jax.vmap(build_coupler)(retain, hopping)

    def compose_step(running, slab_data):
        total_map, total_source = running
        coupler, fresh_source = slab_data
        return (
            (complex_product(coupler, total_map), sandwich(coupler, total_source) + fresh_source),
            None,
        )

    (device_map, device_source), _ = lax.scan(
        compose_step, (couplers[0], source[0]), (couplers[1:], source[1:])
    )

    def hand_over(counter, arriving):
        leaving = sandwich(device_map, arriving) + device_source
        return shifted(leaving, "space", 1)

    entering = lax.fori_loop(
        0, lax.axis_size("space") - 1, hand_over, jnp.zeros_like(device_source)
    )

    def apply_step(arriving, slab_data):
        coupler, fresh_source = slab_data
        leaving = sandwich(coupler, arriving) + fresh_source
        return (leaving, leaving)

    _, greens = lax.scan(apply_step, entering, (couplers, source))
    pair_blocks = greens.reshape(
        greens.shape[0], greens.shape[1], 2, greens.shape[3] * greens.shape[4]
    )
    total_energies = greens.shape[1] * lax.axis_size("energy")
    period = 2 * total_energies
    cosine_lookup, sine_lookup = fourier_tables(period, total_energies)
    green_spectrum = forward_transform(
        lax.all_to_all(pair_blocks, "energy", split_axis=3, concat_axis=1, tiled=True),
        cosine_lookup,
        sine_lookup,
    )
    screen_spectrum = forward_transform(screened, cosine_lookup, sine_lookup)
    real_result = (
        green_spectrum[:, :, 0] * screen_spectrum[:, :, 0]
        - green_spectrum[:, :, 1] * screen_spectrum[:, :, 1]
    )
    imaginary_result = (
        green_spectrum[:, :, 0] * screen_spectrum[:, :, 1]
        + green_spectrum[:, :, 1] * screen_spectrum[:, :, 0]
    )
    real_component = (
        jnp.einsum("wo,cwd->cod", cosine_lookup, real_result, precision=EXACT_PRECISION)
        - jnp.einsum("wo,cwd->cod", sine_lookup, imaginary_result, precision=EXACT_PRECISION)
    ) / period
    imaginary_component = (
        jnp.einsum("wo,cwd->cod", cosine_lookup, imaginary_result, precision=EXACT_PRECISION)
        + jnp.einsum("wo,cwd->cod", sine_lookup, real_result, precision=EXACT_PRECISION)
    ) / period
    self_energy = jnp.stack([real_component, imaginary_component], axis=2)
    return (greens, self_energy)


def solution(mesh):
    placed = (
        P("space", "energy"),
        P("space", "energy", None, None, None),
        P("space", "energy", None, None, None),
        P("space", None, None, "energy"),
    )
    return jax.shard_map(
        body,
        mesh=mesh,
        in_specs=placed,
        out_specs=(P("space", "energy", None, None, None), P("space", None, None, "energy")),
        check_vma=False,
    )
```

profile of v0, /device:TPU:0, one launch (start us, length us, event | category | flops | bytes accessed | tf_op | source)
XLA Modules:
  0.0 140.6 jit_solution(247373426349361048)
XLA Ops:
  0.6 1.1 slice_multiply_fusion
  1.7 0.9 fusion.56
  5.5 0.9 maximum_add_fusion.3
  6.4 27.3 %while.8 = (s32[]{:T(128)}, f32[1,2,128,128]{3,2,1,0:T(8,128)S(1)}, f32[1,2,128,128]{3,2,1,0:T(8,128)S(1)}, f32[1,2,128,128]{3,2,1,0:T(8,128)S(1)}, s32[]{:T(128)}) while((s32[]{:T(128)}, f32[1,2,128,128]{3,2,1,0:T(8,128)S(1)}, f32[1,2,128,128]{3,2,1,0:T(8,128)S(1)}, f32[1,2,128,128]{3,2,1,0:T(8,128)S(1)}, s32[]{:T(128)}) %tuple.44), condition=%wide.region_1.2_spmd, body=%wide.region_0.1_spmd.sunk | while | flops 201457664 | bytes 2752613 | solution.py:85
  8.4 5.0 %collective-permute-start = (f32[1,2,128,128]{3,2,1,0:T(8,128)S(1)}, f32[1,2,128,128]{3,2,1,0:T(8,128)S(1)}, u32[]{:S(2)}, u32[]{:S(2)}) collective-permute-start(f32[1,2,128,128]{3,2,1,0:T(8,128)S(1)} %maximum_add_fusion.6), channel_id=1, source_target_pairs={{0,8},{8,16},{16,24},{1,9},{9,17},{17,25},{2,10},{10,18},{18,26},{... | collective-permute-start | bytes 393224 | tf_op jit(solution)/shard_map/while/body/eval_jaxpr/ppermute | solution.py:13
  13.4 2.7 %collective-permute-done = f32[1,2,128,128]{3,2,1,0:T(8,128)S(1)} collective-permute-done((f32[1,2,128,128]{3,2,1,0:T(8,128)S(1)}, f32[1,2,128,128]{3,2,1,0:T(8,128)S(1)}, u32[]{:S(2)}, u32[]{:S(2)}) %collective-permute-start) | collective-permute-done | bytes 131104 | tf_op jit(solution)/shard_map/while/body/eval_jaxpr/ppermute | solution.py:13
  18.0 4.4 %collective-permute-start = (f32[1,2,128,128]{3,2,1,0:T(8,128)S(1)}, f32[1,2,128,128]{3,2,1,0:T(8,128)S(1)}, u32[]{:S(2)}, u32[]{:S(2)}) collective-permute-start(f32[1,2,128,128]{3,2,1,0:T(8,128)S(1)} %maximum_add_fusion.6), channel_id=1, source_target_pairs={{0,8},{8,16},{16,24},{1,9},{9,17},{17,25},{2,10},{10,18},{18,26},{... | collective-permute-start | bytes 393224 | tf_op jit(solution)/shard_map/while/body/eval_jaxpr/ppermute | solution.py:13
  22.4 2.5 %collective-permute-done = f32[1,2,128,128]{3,2,1,0:T(8,128)S(1)} collective-permute-done((f32[1,2,128,128]{3,2,1,0:T(8,128)S(1)}, f32[1,2,128,128]{3,2,1,0:T(8,128)S(1)}, u32[]{:S(2)}, u32[]{:S(2)}) %collective-permute-start) | collective-permute-done | bytes 131104 | tf_op jit(solution)/shard_map/while/body/eval_jaxpr/ppermute | solution.py:13
  26.9 4.4 %collective-permute-start = (f32[1,2,128,128]{3,2,1,0:T(8,128)S(1)}, f32[1,2,128,128]{3,2,1,0:T(8,128)S(1)}, u32[]{:S(2)}, u32[]{:S(2)}) collective-permute-start(f32[1,2,128,128]{3,2,1,0:T(8,128)S(1)} %maximum_add_fusion.6), channel_id=1, source_target_pairs={{0,8},{8,16},{16,24},{1,9},{9,17},{17,25},{2,10},{10,18},{18,26},{... | collective-permute-start | bytes 393224 | tf_op jit(solution)/shard_map/while/body/eval_jaxpr/ppermute | solution.py:13
  31.2 2.5 %collective-permute-done = f32[1,2,128,128]{3,2,1,0:T(8,128)S(1)} collective-permute-done((f32[1,2,128,128]{3,2,1,0:T(8,128)S(1)}, f32[1,2,128,128]{3,2,1,0:T(8,128)S(1)}, u32[]{:S(2)}, u32[]{:S(2)}) %collective-permute-start) | collective-permute-done | bytes 131104 | tf_op jit(solution)/shard_map/while/body/eval_jaxpr/ppermute | solution.py:13
  33.7 7.6 %while.28 = (s32[]{:T(128)}, f32[1,2,128,128]{3,2,1,0:T(8,128)S(1)}, f32[2,1,2,128,128]{4,3,2,1,0:T(8,128)S(1)}, f32[2,1,2,128,128]{4,3,2,1,0:T(8,128)S(1)}, f32[2,1,2,128,128]{4,3,2,1,0:T(8,128)}, /*index=5*/s32[]{:T(128)}) while((s32[]{:T(128)}, f32[1,2,128,128]{3,2,1,0:T(8,128)S(1)}, f32[2,1,2,128,128]{4,3,2,1,0:T(8,128)S(1)}, ...), condition=%wide.region_3.4_spmd, body=%wide.region_2.3_spmd.sunk | while | flops 201523200 | bytes 2883665 | solution.py:94
  35.7 0.9 fusion.238
  36.6 0.9 maximum_add_fusion.7
  39.5 0.9 fusion.238
  40.4 0.9 maximum_add_fusion.7
  41.4 11.3 %copy.10 = f32[2,1,2,128,128]{0,2,4,3,1:T(2,128)} copy(f32[2,1,2,128,128]{4,3,2,1,0:T(8,128)S(1)} %get-tuple-element.70) | data formatting | bytes 524288 | tf_op jit(solution)/shard_map/while | solution.py:94
  52.7 25.8 %reshape.358 = f32[8,1,8192]{2,1,0:T(1,128)} reshape(f32[16384,1,2,2]{3,2,1,0:T(2,128)} %bitcast.277) | data formatting | bytes 524288
  78.6 3.7 %all-to-all-start = ((f32[8,1,8192]{2,1,0:T(1,128)}), f32[8,1,8192]{2,1,0:T(1,128)S(1)}, u32[]{:S(2)}, u32[]{:S(2)}) async-start(f32[8,1,8192]{2,1,0:T(1,128)} %reshape.358), calls=%async_computation | async-start | bytes 524288 | tf_op jit(solution)/shard_map/all_to_all | solution.py:102
  82.5 0.5 fusion.60
  83.0 0.5 fusion.59
  83.5 0.5 fusion.43
  83.9 0.5 fusion.45
  84.4 4.8 %all-to-all-done = f32[8,1,8192]{2,1,0:T(1,128)S(1)} async-done(((f32[8,1,8192]{2,1,0:T(1,128)}), f32[8,1,8192]{2,1,0:T(1,128)S(1)}, u32[]{:S(2)}, u32[]{:S(2)}) %all-to-all-start) | async-done | bytes 262176 | tf_op jit(solution)/shard_map/all_to_all | solution.py:102
  89.2 0.5 broadcast.72
  89.7 1.3 reduce
  91.0 32.2 %reshape.359 = f32[16384,1,2,2]{3,2,1,0:T(2,128)} reshape(f32[8,8192]{1,0:T(8,128)S(1)} %reduce) | data formatting | bytes 524288
  123.1 13.4 %copy.15 = f32[2,1,2,8,2048]{4,3,0,2,1:T(8,128)S(1)} copy(f32[2,1,2,8,2048]{0,2,4,3,1:T(2,128)} %bitcast.276) | data formatting | bytes 524288 | tf_op jit(solution)/shard_map/all_to_all | solution.py:102
  136.5 0.5 fusion.61
  137.0 0.5 fusion.62
  137.5 0.5 fusion.46
  138.0 0.5 multiply_subtract_fusion
  139.7 0.9 copy.14
  (72 shorter events, 13.7 us)
Async XLA Ops:
  8.4 7.7 %collective-permute-start = (f32[1,2,128,128]{3,2,1,0:T(8,128)S(1)}, f32[1,2,128,128]{3,2,1,0:T(8,128)S(1)}, u32[]{:S(2)}, u32[]{:S(2)}) collective-permute-start(f32[1,2,128,128]{3,2,1,0:T(8,128)S(1)} %maximum_add_fusion.6), channel_id=1, source_target_pairs={{0,8},{8,16},{16,24},{1,9},{9,17},{17,25},{2,10},{10,18},{18,26},{... | collective-permute-start | bytes 393224 | tf_op jit(solution)/shard_map/while/body/eval_jaxpr/ppermute | solution.py:13
  18.0 6.9 %collective-permute-start = (f32[1,2,128,128]{3,2,1,0:T(8,128)S(1)}, f32[1,2,128,128]{3,2,1,0:T(8,128)S(1)}, u32[]{:S(2)}, u32[]{:S(2)}) collective-permute-start(f32[1,2,128,128]{3,2,1,0:T(8,128)S(1)} %maximum_add_fusion.6), channel_id=1, source_target_pairs={{0,8},{8,16},{16,24},{1,9},{9,17},{17,25},{2,10},{10,18},{18,26},{... | collective-permute-start | bytes 393224 | tf_op jit(solution)/shard_map/while/body/eval_jaxpr/ppermute | solution.py:13
  26.9 6.9 %collective-permute-start = (f32[1,2,128,128]{3,2,1,0:T(8,128)S(1)}, f32[1,2,128,128]{3,2,1,0:T(8,128)S(1)}, u32[]{:S(2)}, u32[]{:S(2)}) collective-permute-start(f32[1,2,128,128]{3,2,1,0:T(8,128)S(1)} %maximum_add_fusion.6), channel_id=1, source_target_pairs={{0,8},{8,16},{16,24},{1,9},{9,17},{17,25},{2,10},{10,18},{18,26},{... | collective-permute-start | bytes 393224 | tf_op jit(solution)/shard_map/while/body/eval_jaxpr/ppermute | solution.py:13
  41.4 37.2 %copy-start = (f32[2,1,2,128,128]{4,3,2,1,0:T(8,128)}, f32[2,1,2,128,128]{4,3,2,1,0:T(8,128)S(1)}, u32[]{:S(2)}) copy-start(f32[2,1,2,128,128]{4,3,2,1,0:T(8,128)S(1)} %get-tuple-element.70) | copy-start | bytes 786436
  41.4 40.9 %copy-start.1 = (f32[2,8,2,2048]{3,2,1,0:T(2,128)S(1)}, f32[2,8,2,2048]{3,2,1,0:T(2,128)}, u32[]{:S(2)}) copy-start(f32[2,8,2,2048]{3,2,1,0:T(2,128)} %param.11) | copy-start | bytes 786436
  78.6 10.6 %all-to-all-start = ((f32[8,1,8192]{2,1,0:T(1,128)}), f32[8,1,8192]{2,1,0:T(1,128)S(1)}, u32[]{:S(2)}, u32[]{:S(2)}) async-start(f32[8,1,8192]{2,1,0:T(1,128)} %reshape.358), calls=%async_computation | async-start | bytes 524288 | tf_op jit(solution)/shard_map/all_to_all | solution.py:102
where the time goes:
time: 141 us
  local copies, waits for them, and re-layouts  84.4 us (60%)
  starting transfers between devices  17.4 us (12%)
  matrix products  17.2 us (12%)
  waiting for transfers between devices  12.5 us (9%)
  other arithmetic  7.99 us (6%)
    unnamed x7, local copies, waits for them, and re-layouts  58.9 us
    all_to_all x2, local copies, waits for them, and re-layouts, body(): lax.all_to_all(pair_blocks, 'energy', split_axis=3, concat_axis=1, tiled=...  13.9 us
    ppermute x3, starting transfers between devices, shifted(): lax.ppermute(value, axis, [(source, source + steps) for source in range(i...  13.7 us
    while x1, local copies, waits for them, and re-layouts, body(): _, greens = lax.scan(apply_step, entering, (couplers, source))  11.3 us
    ppermute x3, waiting for transfers between devices, shifted(): lax.ppermute(value, axis, [(source, source + steps) for source in range(i...  7.72 us
    all_to_all x1, waiting for transfers between devices, body(): lax.all_to_all(pair_blocks, 'energy', split_axis=3, concat_axis=1, tiled=...  4.77 us
    all_to_all x1, starting transfers between devices, body(): lax.all_to_all(pair_blocks, 'energy', split_axis=3, concat_axis=1, tiled=...  3.72 us
  transfers between devices with their start and end apart: 4, of which 4 were waited for; matrix products, arithmetic and copies ran while one was open for 1% of the time, Pallas kernels for 0%

commit v1 on v0

--- a/solution.py
+++ b/solution.py
@@ -99,7 +99,12 @@
     period = 2 * total_energies
     cosine_lookup, sine_lookup = fourier_tables(period, total_energies)
     green_spectrum = forward_transform(
-        lax.all_to_all(pair_blocks, "energy", split_axis=3, concat_axis=1, tiled=True),
+        jnp.concatenate(
+            lax.all_to_all(
+                jnp.stack(jnp.split(pair_blocks, lax.axis_size("energy"), axis=3)), "energy", 0, 0
+            ),
+            axis=1,
+        ),
         cosine_lookup,
         sine_lookup,
     )

time: 141 us -> 57.8 us (0.41)
  local copies, waits for them, and re-layouts: 84.4 us -> 7.79 us
  other arithmetic: 7.99 us -> 1.33 us
    unnamed x7 -> x16, local copies, waits for them, and re-layouts: 58.9 us -> 6.59 us
    all_to_all x2 -> x1, local copies, waits for them, and re-layouts: 13.9 us -> 0.16 us  [body(): lax.all_to_all(jnp.stack(jnp.split(pair_blocks, lax.axis_size('energy'),...]
    while x1 -> x0, local copies, waits for them, and re-layouts: 11.3 us -> none  [body(): _, greens = lax.scan(apply_step, entering, (couplers, source))]
    add x2, other arithmetic: 1.85 us -> 0.03 us  [apply_step(): leaving = sandwich(coupler, arriving) + fresh_source]
    dynamic_update_slice x2, other arithmetic: 1.85 us -> 0.04 us  [body(): _, greens = lax.scan(apply_step, entering, (couplers, source))]
  transfers between devices with their start and end apart: 4 -> 4, of which waited for: 4 -> 4; matrix products, arithmetic and copies ran while one was open for 1% -> 4% of each run, Pallas kernels for 0% -> 0%
where the time goes in v1:
time: 57.8 us; the launch traced here: 57.5 us
  starting transfers between devices  17.6 us (30%)
  matrix products  17.1 us (30%)
  waiting for transfers between devices  12.5 us (22%)
  local copies, waits for them, and re-layouts  7.79 us (13%)
  other arithmetic  1.33 us (2%)
  between operations  0.92 us (2%)
    ppermute x3, starting transfers between devices, shifted(): lax.ppermute(value, axis, [(source, source + steps) for source in range(i...  13.7 us
    ppermute x3, waiting for transfers between devices, shifted(): lax.ppermute(value, axis, [(source, source + steps) for source in range(i...  7.71 us
    unnamed x16, local copies, waits for them, and re-layouts  6.59 us
    all_to_all x1, waiting for transfers between devices, body(): lax.all_to_all(jnp.stack(jnp.split(pair_blocks, lax.axis_size('energy'),...  4.77 us
    all_to_all x1, starting transfers between devices, body(): lax.all_to_all(jnp.stack(jnp.split(pair_blocks, lax.axis_size('energy'),...  3.86 us
    dot_general x6, matrix products, times_dagger(): jnp.einsum('eij,ekj->eik', left_matrix[:, 1], right_matrix[:, 1], precisi...  1.62 us
    dot_general x6, matrix products, times_dagger(): jnp.einsum('eij,ekj->eik', left_matrix[:, 0], right_matrix[:, 1], precisi...  1.61 us
    dot_general x6, matrix products, times_dagger(): jnp.einsum('eij,ekj->eik', left_matrix[:, 0], right_matrix[:, 0], precisi...  1.6 us
  transfers between devices with their start and end apart: 4, of which 4 were waited for; matrix products, arithmetic and copies ran while one was open for 4% of the time, Pallas kernels for 0%

profile of v1, /device:TPU:0, one launch (start us, length us, event | category | flops | bytes accessed | tf_op | source)
XLA Modules:
  0.0 57.5 jit_solution(1096530413958129201)
XLA Ops:
  0.7 0.6 %copy-done.3 = f32[2,1]{0,1:T(1,128)S(1)} copy-done((f32[2,1]{0,1:T(1,128)S(1)}, f32[2,1]{0,1:T(1,128)}, u32[]{:S(2)}) %copy-start.3) | copy-done | bytes 32
  1.3 1.1 %slice_multiply_fusion = (f32[2,1,1,128,128]{4,3,2,1,0:T(8,128)S(1)}, f32[2,1,1,128,128]{4,3,2,1,0:T(8,128)S(1)}) fusion(f32[2,1,2,128,128]{4,3,2,1,0:T(8,128)} %param.9, f32[2]{0:T(128)S(1)} %bitcast.316, f32[128,128]{1,0:T(8,128)S(1)} %fusion.63), kind=kLoop, calls=%fused_computation.101 | loop fusion | flops 98304 | bytes 589832 | tf_op jit(solution)/shard_map/vmap()/mul | solution.py:20
  5.3 27.3 %while.8 = (s32[]{:T(128)}, f32[1,2,128,128]{3,2,1,0:T(8,128)S(1)}, f32[1,2,128,128]{3,2,1,0:T(8,128)S(1)}, f32[1,2,128,128]{3,2,1,0:T(8,128)S(1)}, s32[]{:T(128)}) while((s32[]{:T(128)}, f32[1,2,128,128]{3,2,1,0:T(8,128)S(1)}, f32[1,2,128,128]{3,2,1,0:T(8,128)S(1)}, f32[1,2,128,128]{3,2,1,0:T(8,128)S(1)}, s32[]{:T(128)}) %tuple.51), condition=%wide.region_1.2_spmd, body=%wide.region_0.1_spmd.sunk | while | flops 201457664 | bytes 2752613 | solution.py:85
  7.3 5.0 %collective-permute-start = (f32[1,2,128,128]{3,2,1,0:T(8,128)S(1)}, f32[1,2,128,128]{3,2,1,0:T(8,128)S(1)}, u32[]{:S(2)}, u32[]{:S(2)}) collective-permute-start(f32[1,2,128,128]{3,2,1,0:T(8,128)S(1)} %maximum_add_fusion.6), channel_id=1, source_target_pairs={{0,8},{8,16},{16,24},{1,9},{9,17},{17,25},{2,10},{10,18},{18,26},{... | collective-permute-start | bytes 393224 | tf_op jit(solution)/shard_map/while/body/eval_jaxpr/ppermute | solution.py:13
  12.3 2.7 %collective-permute-done = f32[1,2,128,128]{3,2,1,0:T(8,128)S(1)} collective-permute-done((f32[1,2,128,128]{3,2,1,0:T(8,128)S(1)}, f32[1,2,128,128]{3,2,1,0:T(8,128)S(1)}, u32[]{:S(2)}, u32[]{:S(2)}) %collective-permute-start) | collective-permute-done | bytes 131104 | tf_op jit(solution)/shard_map/while/body/eval_jaxpr/ppermute | solution.py:13
  16.9 4.4 %collective-permute-start = (f32[1,2,128,128]{3,2,1,0:T(8,128)S(1)}, f32[1,2,128,128]{3,2,1,0:T(8,128)S(1)}, u32[]{:S(2)}, u32[]{:S(2)}) collective-permute-start(f32[1,2,128,128]{3,2,1,0:T(8,128)S(1)} %maximum_add_fusion.6), channel_id=1, source_target_pairs={{0,8},{8,16},{16,24},{1,9},{9,17},{17,25},{2,10},{10,18},{18,26},{... | collective-permute-start | bytes 393224 | tf_op jit(solution)/shard_map/while/body/eval_jaxpr/ppermute | solution.py:13
  21.3 2.5 %collective-permute-done = f32[1,2,128,128]{3,2,1,0:T(8,128)S(1)} collective-permute-done((f32[1,2,128,128]{3,2,1,0:T(8,128)S(1)}, f32[1,2,128,128]{3,2,1,0:T(8,128)S(1)}, u32[]{:S(2)}, u32[]{:S(2)}) %collective-permute-start) | collective-permute-done | bytes 131104 | tf_op jit(solution)/shard_map/while/body/eval_jaxpr/ppermute | solution.py:13
  25.8 4.4 %collective-permute-start = (f32[1,2,128,128]{3,2,1,0:T(8,128)S(1)}, f32[1,2,128,128]{3,2,1,0:T(8,128)S(1)}, u32[]{:S(2)}, u32[]{:S(2)}) collective-permute-start(f32[1,2,128,128]{3,2,1,0:T(8,128)S(1)} %maximum_add_fusion.6), channel_id=1, source_target_pairs={{0,8},{8,16},{16,24},{1,9},{9,17},{17,25},{2,10},{10,18},{18,26},{... | collective-permute-start | bytes 393224 | tf_op jit(solution)/shard_map/while/body/eval_jaxpr/ppermute | solution.py:13
  30.1 2.5 %collective-permute-done = f32[1,2,128,128]{3,2,1,0:T(8,128)S(1)} collective-permute-done((f32[1,2,128,128]{3,2,1,0:T(8,128)S(1)}, f32[1,2,128,128]{3,2,1,0:T(8,128)S(1)}, u32[]{:S(2)}, u32[]{:S(2)}) %collective-permute-start) | collective-permute-done | bytes 131104 | tf_op jit(solution)/shard_map/while/body/eval_jaxpr/ppermute | solution.py:13
  32.6 4.0 %while.28 = (s32[]{:T(128)}, f32[1,2,128,128]{3,2,1,0:T(8,128)S(1)}, f32[2,1,2,128,128]{4,3,2,1,0:T(8,128)S(1)}, f32[2,1,2,128,128]{4,3,2,1,0:T(8,128)S(1)}, f32[2,1,2,128,128]{4,3,2,1,0:T(8,128)S(1)}, /*index=5*/s32[]{:T(128)}) while((s32[]{:T(128)}, f32[1,2,128,128]{3,2,1,0:T(8,128)S(1)}, f32[2,1,2,128,128]{4,3,2,1,0:T(8,128)S(1)}, ...), condition=%wide.region_3.4_spmd, body=%wide.region_2.3_spmd.sunk | while | flops 201523200 | bytes 2883673 | solution.py:94
  36.8 0.5 copy-done.2
  37.4 0.6 %fusion.77 = f32[8,2,1,2,2048]{4,1,3,2,0:T(2,128)} fusion(f32[2,1,2,2048]{3,2,0,1:T(2,128)S(1)} %get-tuple-element.103), kind=kLoop, calls=%fused_computation.136 | loop fusion | bytes 65536
  38.0 0.6 %fusion.76 = f32[8,2,1,2,2048]{4,1,3,2,0:T(2,128)} fusion(f32[8,2,1,2,2048]{4,1,3,2,0:T(2,128)} %fusion.77, f32[2,1,2,2048]{3,2,0,1:T(2,128)S(1)} %get-tuple-element.102), kind=kLoop, calls=%fused_computation.134 | loop fusion | bytes 65536
  38.7 0.6 %fusion.75 = f32[8,2,1,2,2048]{4,1,3,2,0:T(2,128)} fusion(f32[8,2,1,2,2048]{4,1,3,2,0:T(2,128)} %fusion.76, f32[2,1,2,2048]{3,2,0,1:T(2,128)S(1)} %get-tuple-element.101), kind=kLoop, calls=%fused_computation.132 | loop fusion | bytes 65536
  39.3 0.6 %fusion.74 = f32[8,2,1,2,2048]{4,1,3,2,0:T(2,128)} fusion(f32[8,2,1,2,2048]{4,1,3,2,0:T(2,128)} %fusion.75, f32[2,1,2,2048]{3,2,0,1:T(2,128)S(1)} %get-tuple-element.100), kind=kLoop, calls=%fused_computation.130 | loop fusion | bytes 65536
  39.9 0.6 %fusion.73 = f32[8,2,1,2,2048]{4,1,3,2,0:T(2,128)} fusion(f32[8,2,1,2,2048]{4,1,3,2,0:T(2,128)} %fusion.74, f32[2,1,2,2048]{3,2,0,1:T(2,128)S(1)} %get-tuple-element.99), kind=kLoop, calls=%fused_computation.128 | loop fusion | bytes 65536
  40.6 0.6 %fusion.72 = f32[8,2,1,2,2048]{4,1,3,2,0:T(2,128)} fusion(f32[8,2,1,2,2048]{4,1,3,2,0:T(2,128)} %fusion.73, f32[2,1,2,2048]{3,2,0,1:T(2,128)S(1)} %get-tuple-element.98), kind=kLoop, calls=%fused_computation.126 | loop fusion | bytes 65536
  41.2 0.6 %fusion.71 = f32[8,2,1,2,2048]{4,1,3,2,0:T(2,128)} fusion(f32[8,2,1,2,2048]{4,1,3,2,0:T(2,128)} %fusion.72, f32[2,1,2,2048]{3,2,0,1:T(2,128)S(1)} %get-tuple-element.97), kind=kLoop, calls=%fused_computation.124 | loop fusion | bytes 65536
  41.9 0.6 %fusion.70 = f32[8,2,1,2,2048]{4,1,3,2,0:T(2,128)} fusion(f32[8,2,1,2,2048]{4,1,3,2,0:T(2,128)} %fusion.71, f32[2,1,2,2048]{3,2,0,1:T(2,128)S(1)} %get-tuple-element.96), kind=kLoop, calls=%fused_computation.122 | loop fusion | bytes 65536 | tf_op jit(solution)/shard_map/stack | solution.py:104
  42.5 3.9 %all-to-all-start = ((f32[8,2,1,2,2048]{4,1,3,2,0:T(2,128)}), f32[8,2,1,2,2048]{4,1,3,2,0:T(2,128)S(1)}, u32[]{:S(2)}, u32[]{:S(2)}) async-start(f32[8,2,1,2,2048]{4,1,3,2,0:T(2,128)} %fusion.70), calls=%async_computation | async-start | bytes 524288 | tf_op jit(solution)/shard_map/all_to_all | solution.py:103
  46.6 0.5 fusion.60
  47.1 0.5 fusion.59
  47.5 0.5 fusion.43
  48.0 0.5 fusion.45
  48.5 4.8 %all-to-all-done = f32[8,2,1,2,2048]{4,1,3,2,0:T(2,128)S(1)} async-done(((f32[8,2,1,2,2048]{4,1,3,2,0:T(2,128)}), f32[8,2,1,2,2048]{4,1,3,2,0:T(2,128)S(1)}, u32[]{:S(2)}, u32[]{:S(2)}) %all-to-all-start) | async-done | bytes 262176 | tf_op jit(solution)/shard_map/all_to_all | solution.py:103
  53.4 0.5 fusion.61
  53.9 0.5 fusion.62
  54.4 0.5 fusion.46
  54.9 0.5 multiply_subtract_fusion
  56.0 0.3 fusion.48
  56.3 0.3 fusion.50
  56.6 0.9 %copy.21 = f32[2,8,2,2048]{3,2,1,0:T(2,128)} copy(f32[2,8,2,2048]{3,1,0,2:T(8,128)S(1)} %pad_maximum_fusion.1) | data formatting | bytes 524288
  (81 shorter events, 13.6 us)
Async XLA Ops:
  0.6 0.7 %copy-start.3 = (f32[2,1]{0,1:T(1,128)S(1)}, f32[2,1]{0,1:T(1,128)}, u32[]{:S(2)}) copy-start(f32[2,1]{0,1:T(1,128)} %param.8) | copy-start | bytes 28
  1.3 1.1 %copy-start = (f32[2,1,2,128,128]{4,3,2,1,0:T(8,128)S(1)}, f32[2,1,2,128,128]{4,3,2,1,0:T(8,128)}, u32[]{:S(2)}) copy-start(f32[2,1,2,128,128]{4,3,2,1,0:T(8,128)} %param.10) | copy-start | bytes 786436
  7.3 7.7 %collective-permute-start = (f32[1,2,128,128]{3,2,1,0:T(8,128)S(1)}, f32[1,2,128,128]{3,2,1,0:T(8,128)S(1)}, u32[]{:S(2)}, u32[]{:S(2)}) collective-permute-start(f32[1,2,128,128]{3,2,1,0:T(8,128)S(1)} %maximum_add_fusion.6), channel_id=1, source_target_pairs={{0,8},{8,16},{16,24},{1,9},{9,17},{17,25},{2,10},{10,18},{18,26},{... | collective-permute-start | bytes 393224 | tf_op jit(solution)/shard_map/while/body/eval_jaxpr/ppermute | solution.py:13
  16.9 6.9 %collective-permute-start = (f32[1,2,128,128]{3,2,1,0:T(8,128)S(1)}, f32[1,2,128,128]{3,2,1,0:T(8,128)S(1)}, u32[]{:S(2)}, u32[]{:S(2)}) collective-permute-start(f32[1,2,128,128]{3,2,1,0:T(8,128)S(1)} %maximum_add_fusion.6), channel_id=1, source_target_pairs={{0,8},{8,16},{16,24},{1,9},{9,17},{17,25},{2,10},{10,18},{18,26},{... | collective-permute-start | bytes 393224 | tf_op jit(solution)/shard_map/while/body/eval_jaxpr/ppermute | solution.py:13
  25.8 6.9 %collective-permute-start = (f32[1,2,128,128]{3,2,1,0:T(8,128)S(1)}, f32[1,2,128,128]{3,2,1,0:T(8,128)S(1)}, u32[]{:S(2)}, u32[]{:S(2)}) collective-permute-start(f32[1,2,128,128]{3,2,1,0:T(8,128)S(1)} %maximum_add_fusion.6), channel_id=1, source_target_pairs={{0,8},{8,16},{16,24},{1,9},{9,17},{17,25},{2,10},{10,18},{18,26},{... | collective-permute-start | bytes 393224 | tf_op jit(solution)/shard_map/while/body/eval_jaxpr/ppermute | solution.py:13
  36.7 0.7 %copy-start.2 = (f32[2,1,2,128,128]{4,3,2,1,0:T(8,128)}, f32[2,1,2,128,128]{4,3,2,1,0:T(8,128)S(1)}, u32[]{:S(2)}) copy-start(f32[2,1,2,128,128]{4,3,2,1,0:T(8,128)S(1)} %get-tuple-element.70) | copy-start | bytes 786436
  42.5 3.9 %copy-start.1 = (f32[2,8,2,2048]{3,2,1,0:T(2,128)S(1)}, f32[2,8,2,2048]{3,2,1,0:T(2,128)}, u32[]{:S(2)}) copy-start(f32[2,8,2,2048]{3,2,1,0:T(2,128)} %param.11) | copy-start | bytes 786436
  42.5 10.8 %all-to-all-start = ((f32[8,2,1,2,2048]{4,1,3,2,0:T(2,128)}), f32[8,2,1,2,2048]{4,1,3,2,0:T(2,128)S(1)}, u32[]{:S(2)}, u32[]{:S(2)}) async-start(f32[8,2,1,2,2048]{4,1,3,2,0:T(2,128)} %fusion.70), calls=%async_computation | async-start | bytes 524288 | tf_op jit(solution)/shard_map/all_to_all | solution.py:103
